TPU v7x, 128 devices: a whole 4x4x4 slice. The times are simulated.
128 devices in a mesh: row: 8 (over x, z_lo), col: 16 (over y, z_hi, core).
Axes of the slice: x: 4, y: 4, z: 4 (z_hi: 2, z_lo: 2; z = z_hi * 2 + z_lo), core: 2. Of those that a mesh axis runs over, the one named last changes fastest.
Arguments:
- gate_pre: bfloat16 [2048, 26624], P('col', 'row'), may hold values from -6 to 6
- up_pre: bfloat16 [2048, 26624], P('col', 'row'), may hold values from -6 to 6
- residual: bfloat16 [2048, 16384], P('row', 'col'), may hold values from -6 to 6
- base_weight: bfloat16 [26624, 16384], P('row', 'col'), may hold values from -0.0390625 to 0.0390625
- perturb: bfloat16 [26624, 16384], P('row', 'col'), may hold values from -0.0390625 to 0.0390625
- exponents: int32 [208, 16384], P('row', 'col'), may hold values from -2 to 1
Outputs:
- plus_out: bfloat16 [2048, 16384], P('row', 'col')
- minus_out: bfloat16 [2048, 16384], P('row', 'col')
All inputs are finite; a program needn't handle non-finite values.
Results may differ from a plain program's by a relative error of at most 0.004.
Values may be sent and summed in bfloat16 or wider, within the bound.
A program may use at most 128 MiB of HBM per device.

v0:
```python
import jax
import jax.numpy as jnp
from jax import lax
from jax.sharding import Mesh
from jax.sharding import PartitionSpec as P

ROW = ("row_0", "row_1")


step_size = 0.25


def own_rows(so_far, axes):
    for axis in axes:
        so_far = lax.psum_scatter(so_far, axis, scatter_dimension=0, tiled=True)
    return so_far


def swiglu(gate_part, up_part):
    return (jax.nn.silu(gate_part.astype(jnp.float32)) * up_part.astype(jnp.float32)).astype(
        jnp.bfloat16
    )


def on_device(gate_pre, up_pre, residual, base_weight, perturb, exponents):
    hidden = lax.all_gather(swiglu(gate_pre, up_pre), "col", axis=0, tiled=True)
    group_size = base_weight.shape[0] // exponents.shape[0]
    factor = jnp.repeat(jnp.exp2(exponents.astype(jnp.float32)), group_size, axis=0)
    shift = step_size * factor * perturb.astype(jnp.float32)
    weight_full = base_weight.astype(jnp.float32)
    plus_weight = (weight_full + shift).astype(jnp.bfloat16)
    minus_weight = (weight_full - shift).astype(jnp.bfloat16)
    stream = residual.astype(jnp.float32)
    stacked = jnp.concatenate([plus_weight, minus_weight], axis=1)
    summed = own_rows(jnp.dot(hidden, stacked, preferred_element_type=jnp.float32), ROW)
    columns = base_weight.shape[1]
    plus_sum = summed[:, :columns]
    minus_sum = summed[:, columns:]
    plus_out = (stream + plus_sum).astype(jnp.bfloat16)
    minus_out = (stream + minus_sum).astype(jnp.bfloat16)
    return (plus_out, minus_out)


def solution(mesh):
    finer = Mesh(mesh.devices.reshape(4, 2, mesh.shape["col"]), ("row_0", "row_1", "col"))
    in_specs = (
        P("col", ROW),
        P("col", ROW),
        P(ROW, "col"),
        P(ROW, "col"),
        P(ROW, "col"),
        P(ROW, "col"),
    )
    out_specs = (P(ROW, "col"), P(ROW, "col"))
    return jax.shard_map(
        on_device, mesh=finer, in_specs=in_specs, out_specs=out_specs, check_vma=False
    )
```

profile of v0, /device:TPU:1, one launch (start us, length us, event | category | flops | bytes accessed | tf_op | source)
XLA Modules:
  0.0 360.9 jit_solution(1346917091632960387)
XLA Ops:
  7.2 0.0 all-gather.2.cloned.1.call-start
  7.2 2.8 fusion.10
  10.0 0.0 all-gather.2.cloned.1.call-update
  10.1 0.0 reduce-scatter.3.cloned.1.call-start
  10.1 0.9 exponential_multiply_fusion
  11.0 10.9 %fusion = (bf16[3328,1024]{1,0:T(8,128)(2,1)}, bf16[3328,1024]{1,0:T(8,128)(2,1)}) fusion(bf16[3328,1024]{1,0:T(8,128)(2,1)} %param.9, bf16[3328,1024]{1,0:T(8,128)(2,1)} %param.10, f32[26,1024]{1,0:T(8,128)S(1)} %exponential_multiply_fusion), kind=kLoop, calls=%fused_computation.2 | loop fusion | flops 23855104 | bytes 27369472 | tf_op jit(solution)/shard_map/convert_element_type | solution.py:31
  22.0 87.9 %all-gather.2.cloned.1.call-done = bf16[2048,3328]{1,0:T(8,128)(2,1)} async-done(((bf16[128,3328]{1,0:T(8,128)(2,1)}), bf16[2048,3328]{1,0:T(8,128)(2,1)}) %all-gather.2.cloned.1.call-update) | async-done | bytes 13631504 | tf_op jit(solution)/shard_map/all_gather | solution.py:26
  109.9 37.3 %fusion.2 = f32[2048,2048]{1,0:T(8,128)} fusion(bf16[2048,3328]{1,0:T(8,128)(2,1)} %all-gather.2.cloned.1.call-done, bf16[3328,1024]{1,0:T(8,128)(2,1)} %get-tuple-element.3, bf16[3328,1024]{1,0:T(8,128)(2,1)} %get-tuple-element.2), kind=kOutput, calls=%fused_computation.4 | convolution fusion | flops 27944550400 | bytes 44040192 | tf_op jit(solution)/shard_map/dot_general | solution.py:35
  147.2 0.0 copy-start
  147.2 0.0 reduce-scatter.3.cloned.1.call-update
  147.2 0.0 reduce-scatter.5.cloned.1.call-start
  147.2 145.2 %reduce-scatter.3.cloned.1.call-done = f32[512,2048]{1,0:T(8,128)} async-done(((f32[2048,2048]{1,0:T(8,128)}), f32[512,2048]{1,0:T(8,128)}) %reduce-scatter.3.cloned.1.call-update) | async-done | bytes 4194320 | tf_op jit(solution)/shard_map/reduce_scatter | solution.py:15
  292.4 0.0 reduce-scatter.5.cloned.1.call-update
  292.5 59.1 %reduce-scatter.5.cloned.1.call-done = f32[256,2048]{1,0:T(8,128)} async-done(((f32[512,2048]{1,0:T(8,128)}), f32[256,2048]{1,0:T(8,128)}) %reduce-scatter.5.cloned.1.call-update) | async-done | bytes 2097168 | tf_op jit(solution)/shard_map/reduce_scatter | solution.py:15
  351.6 0.0 copy-done
  351.6 2.8 fusion.12
Async XLA Ops:
  7.2 102.7 %all-gather.2.cloned.1.call-start = ((), (), s32[]{:S(2)}) async-start(), calls=%async_computation.2 | async-start | bytes 14483456 | tf_op jit(solution)/shard_map/all_gather | solution.py:26
  10.1 282.4 %reduce-scatter.3.cloned.1.call-start = ((), (), s32[]{:S(2)}) async-start(), calls=%async_computation.3 | async-start | bytes 20971520 | tf_op jit(solution)/shard_map/reduce_scatter | solution.py:15
  147.2 204.4 %copy-start = (bf16[256,1024]{1,0:T(8,128)(2,1)S(1)}, bf16[256,1024]{1,0:T(8,128)(2,1)}, u32[]{:S(2)}) copy-start(bf16[256,1024]{1,0:T(8,128)(2,1)} %param.8) | copy-start | bytes 1572868
  147.2 204.4 %reduce-scatter.5.cloned.1.call-start = ((), (), s32[]{:S(2)}) async-start(), calls=%async_computation.4 | async-start | bytes 6291456 | tf_op jit(solution)/shard_map/reduce_scatter | solution.py:15
Sparse Core Ops, SparseCore 0:
  10.4 99.4 all-gather.1
  147.3 145.0 reduce-scatter.2
  295.0 56.5 reduce-scatter.4
where the time goes:
time: 361 us
  waiting for transfers between devices  292 us (81%)
  matrix products  37.3 us (10%)
  other arithmetic  17.5 us (5%)
  between operations  13.7 us (4%)
    reduce_scatter x2, waiting for transfers between devices, own_rows(): so_far = lax.psum_scatter(so_far, axis, scatter_dimension=0, tiled=True)  204 us
    all_gather x1, waiting for transfers between devices, on_device(): hidden = lax.all_gather(swiglu(gate_pre, up_pre), 'col', axis=0, tiled=True)  87.9 us
    dot_general x1, matrix products, on_device(): jnp.dot(hidden, stacked, preferred_element_type=jnp.float32)  37.3 us
    convert_element_type x1, other arithmetic, on_device(): plus_weight = (weight_full + shift).astype(jnp.bfloat16)  10.9 us
  transfers between devices with their start and end apart: 3, of which 3 were waited for; matrix products, arithmetic and copies ran while one was open for 3% of the time, Pallas kernels for 0%

commit v1 on v0

v1 whole, which is shorter than its diff:
```python
import functools

import jax
import jax.numpy as jnp
from jax import lax
from jax.experimental import pallas as pl
from jax.experimental.pallas import tpu as pltpu
from jax.sharding import PartitionSpec as P

MESH = pl.DeviceIdType.MESH
STEP_SIZE = 0.25
CHUNKS = 4
ZP, Y_AHEAD, Y_BEHIND, OZ_AHEAD, OZ_BEHIND, Y_FAR, OZ_FAR, SIB = range(8)
N_AG = SIB + 8
FAR, MID, NEAR, ZSUM = 0, 2, 4, 6
N_RS = 7


def kernel(
    gate_hbm, up_hbm, res_ref, base_hbm, pert_hbm, expo_ref,
    plus_ref, minus_ref,
    gate_buf, up_buf, base_buf, pert_buf, factor_ref, hid, weight, part,
    far_in, mid_in, near_in, z_in,
    in_sem, w_sem, ag_send, ag_recv, rs_send, rs_recv,
):
    tokens, depth = gate_buf.shape
    piece = tokens // CHUNKS
    columns = base_buf.shape[2]
    w_rows = base_buf.shape[1]
    w_tiles = depth // w_rows
    tile_n = weight.shape[2]
    n_tiles = weight.shape[0]
    group = depth // expo_ref.shape[0]

    row, col = lax.axis_index("row"), lax.axis_index("col")
    x, zl = row // 2, row % 2
    y, zh, core = col // 4, (col // 2) % 2, col % 2
    step = 2 * core + 3
    back = 5 - 2 * core
    x_ahead, x_behind = (x + step) % 4, (x + back) % 4
    y_ahead, y_behind, y_far = (y + step) % 4, (y + back) % 4, (y + 2) % 4

    def col_of(y_, zh_, core_=core):
        return y_ * 4 + zh_ * 2 + core_

    oz, oc, ozl = 1 - zh, 1 - core, 1 - zl
    zp_dev = (row, col_of(y, oz))
    ya_dev, yb_dev = (row, col_of(y_ahead, zh)), (row, col_of(y_behind, zh))
    sib_dev = (row, col_of(y, zh, oc))
    xa_dev, xb_dev = (x_ahead * 2 + zl, col), (x_behind * 2 + zl, col)
    zl_dev = (x * 2 + ozl, col)

    origins = [
        (y, zh), (y, oz), (y_behind, zh), (y_ahead, zh),
        (y_behind, oz), (y_ahead, oz), (y_far, zh), (y_far, oz),
    ]

    in_copies = [
        pltpu.make_async_copy(gate_hbm, gate_buf, in_sem.at[0]),
        pltpu.make_async_copy(up_hbm, up_buf, in_sem.at[1]),
    ]
    for copy in in_copies:
        copy.start()

    def w_copies(i, slot):
        rows = pl.ds(pl.multiple_of(i * w_rows, w_rows), w_rows)
        return (
            pltpu.make_async_copy(base_hbm.at[rows], base_buf.at[slot], w_sem.at[0, slot]),
            pltpu.make_async_copy(pert_hbm.at[rows], pert_buf.at[slot], w_sem.at[1, slot]),
        )

    for slot in range(2):
        for copy in w_copies(slot, slot):
            copy.start()

    barrier = pltpu.get_barrier_semaphore()
    for dev in (zp_dev, ya_dev, yb_dev, sib_dev, xa_dev, xb_dev, zl_dev):
        pl.semaphore_signal(barrier, inc=1, device_id=dev, device_id_type=MESH)

    def ag(k, kind, origin, dev):
        src = hid.at[k, origin]
        return pltpu.make_async_remote_copy(
            src_ref=src, dst_ref=src, send_sem=ag_send.at[k, kind], recv_sem=ag_recv.at[k, kind],
            device_id=dev, device_id_type=MESH,
        )

    def ag_send_piece(k, kind, place, dev):
        ag(k, kind, col_of(*origins[place]), dev).start()

    def ag_wait(k, kind):
        ag(k, kind, 0, sib_dev).wait_recv()

    def to_sibling(k, place):
        ag_send_piece(k, SIB + place, place, sib_dev)

    def stage0(k):
        ag_send_piece(k, ZP, 0, zp_dev)
        ag_send_piece(k, Y_AHEAD, 0, ya_dev)
        ag_send_piece(k, Y_BEHIND, 0, yb_dev)
        to_sibling(k, 0)

    def stage1(k):
        ag_wait(k, ZP)
        ag_send_piece(k, OZ_AHEAD, 1, ya_dev)
        ag_send_piece(k, OZ_BEHIND, 1, yb_dev)
        to_sibling(k, 1)

    def stage2(k):
        ag_wait(k, Y_AHEAD)
        ag_send_piece(k, Y_FAR, 2, ya_dev)
        to_sibling(k, 2)
        ag_wait(k, Y_BEHIND)
        to_sibling(k, 3)

    def stage3(k):
        ag_wait(k, OZ_AHEAD)
        ag_send_piece(k, OZ_FAR, 4, ya_dev)
        to_sibling(k, 4)
        ag_wait(k, OZ_BEHIND)
        to_sibling(k, 5)

    def stage4(k):
        ag_wait(k, Y_FAR)
        to_sibling(k, 6)
        ag_wait(k, OZ_FAR)
        to_sibling(k, 7)

    def stage5(k):
        for place in range(8):
            ag_wait(k, SIB + place)

    def rs(k, kind, src, dst, dev):
        return pltpu.make_async_remote_copy(
            src_ref=src, dst_ref=dst, send_sem=rs_send.at[k, kind], recv_sem=rs_recv.at[k, kind],
            device_id=dev, device_id_type=MESH,
        )

    def rs_copy(k, kind):
        if kind == ZSUM:
            return rs(k, kind, part.at[k, x * 2 + ozl], z_in.at[k], zl_dev)
        lo = kind % 2
        dest, dst, dev = {
            FAR: ((x + 2) % 4, far_in, xa_dev),
            MID: (x_ahead, mid_in, xa_dev),
            NEAR: (x_behind, near_in, xb_dev),
        }[kind - lo]
        return rs(k, kind, part.at[k, dest * 2 + lo], dst.at[k, lo], dev)

    def f32(value):
        return value.astype(jnp.float32)

    def send_raw(k):
        for kind in (FAR, FAR + 1, NEAR, NEAR + 1):
            rs_copy(k, kind).start()

    def reduce_mid(k):
        for lo in range(2):
            rs_copy(k, FAR + lo).wait_recv()
            dest = x_ahead * 2 + lo
            part[k, dest] = (f32(part[k, dest]) + f32(far_in[k, lo])).astype(jnp.bfloat16)
            rs_copy(k, MID + lo).start()

    def reduce_z(k):
        for lo in range(2):
            rs_copy(k, NEAR + lo).wait_recv()
            rs_copy(k, MID + lo).wait_recv()
        dest = x * 2 + ozl
        total = f32(part[k, dest]) + f32(mid_in[k, ozl]) + f32(near_in[k, ozl])
        part[k, dest] = total.astype(jnp.bfloat16)
        rs_copy(k, ZSUM).start()

    def finish(k):
        rs_copy(k, ZSUM).wait_recv()
        for half in range(2):
            rows = pl.ds(half * piece, piece)
            out_rows = pl.ds(pl.multiple_of(half * tokens + k * piece, piece), piece)
            total = f32(part[k, x * 2 + zl, rows]) + f32(mid_in[k, zl, rows])
            total = total + f32(near_in[k, zl, rows]) + f32(z_in[k, rows])
            stream = f32(res_ref[out_rows])
            plus_ref[out_rows] = (stream + total[:, :columns]).astype(jnp.bfloat16)
            minus_ref[out_rows] = (stream + total[:, columns:]).astype(jnp.bfloat16)

    for copy in in_copies:
        copy.wait()

    def make_hidden(k):
        rows = pl.ds(pl.multiple_of(k * piece, piece), piece)
        gate, up = f32(gate_buf[rows]), f32(up_buf[rows])
        hid[k, col] = (gate / (1.0 + jnp.exp(-gate)) * up).astype(jnp.bfloat16)

    make_hidden(0)
    pl.semaphore_wait(barrier, 7)
    stage0(0)

    @pl.loop(1, CHUNKS)
    def _(k):
        make_hidden(k)

    stage0(1)
    factor_ref[...] = STEP_SIZE * jnp.exp2(expo_ref[...].astype(jnp.float32))

    @pl.loop(0, w_tiles)
    def _(i):
        slot = i % 2
        for copy in w_copies(i, slot):
            copy.wait()
        for part_group in range(w_rows // group):
            rows = pl.ds(part_group * group, group)
            factor = factor_ref[pl.ds(i * (w_rows // group) + part_group, 1)]
            base = f32(base_buf[slot, rows])
            shift = factor * f32(pert_buf[slot, rows])
            plus = (base + shift).astype(jnp.bfloat16)
            minus = (base - shift).astype(jnp.bfloat16)
            out_rows = pl.ds(pl.multiple_of(i * w_rows + part_group * group, group), group)
            for n in range(n_tiles // 2):
                cols = slice(n * tile_n, (n + 1) * tile_n)
                weight[n, out_rows] = plus[:, cols]
                weight[n + n_tiles // 2, out_rows] = minus[:, cols]

        @pl.when(i + 2 < w_tiles)
        def _():
            for copy in w_copies(i + 2, slot):
                copy.start()

        @pl.when(i == 4)
        def _():
            stage1(0)

        @pl.when(i == 6)
        def _():
            stage2(0)

        @pl.when(i == 9)
        def _():
            stage3(0)

    stage4(0)

    @pl.loop(0, CHUNKS)
    def _(k):
        stage5(k)
        more = k + 1 < CHUNKS

        @pl.loop(0, n_tiles)
        def _(n):
            lhs = hid[k].reshape(hid.shape[1] * piece, depth)
            out = jnp.dot(lhs, weight[n], preferred_element_type=jnp.float32)
            cols = pl.ds(pl.multiple_of(n * tile_n, tile_n), tile_n)
            part[k, :, :, cols] = out.astype(jnp.bfloat16).reshape(
                part.shape[1], part.shape[2], tile_n
            )

            @pl.when((n == 1) & more)
            def _():
                stage1(k + 1)

            @pl.when((n == 1) & (k + 2 < CHUNKS))
            def _():
                stage0(k + 2)

            @pl.when((n == 3) & more)
            def _():
                stage2(k + 1)

            @pl.when((n == 6) & more)
            def _():
                stage3(k + 1)

        send_raw(k)

        @pl.when(k >= 1)
        def _():
            reduce_z(k - 1)

        @pl.when(more)
        def _():
            stage4(k + 1)

        reduce_mid(k)

        @pl.when(k >= 2)
        def _():
            finish(k - 2)

    reduce_z(CHUNKS - 1)
    finish(CHUNKS - 2)
    finish(CHUNKS - 1)

    @pl.loop(0, CHUNKS)
    def _(k):
        for kind in range(N_AG):
            ag(k, kind, 0, sib_dev).wait_send()
        for kind in range(N_RS):
            rs_copy(k, kind).wait_send()


def on_device(gate_pre, up_pre, residual, base_weight, perturb, exponents):
    tokens, depth = gate_pre.shape
    columns = base_weight.shape[1]
    n_col, n_row = 16, 8
    piece = tokens // CHUNKS
    w_rows, tile_n = 256, 256
    bf16 = jnp.bfloat16
    out = jax.ShapeDtypeStruct(residual.shape, bf16)
    any_spec = pl.BlockSpec(memory_space=pl.ANY)
    vmem_spec = pl.BlockSpec(memory_space=pltpu.VMEM)
    rows_out = n_col // n_row * piece
    return pl.pallas_call(
        kernel,
        out_shape=(out, out),
        in_specs=[any_spec, any_spec, vmem_spec, any_spec, any_spec, vmem_spec],
        out_specs=(vmem_spec, vmem_spec),
        scratch_shapes=[
            pltpu.VMEM((tokens, depth), bf16),
            pltpu.VMEM((tokens, depth), bf16),
            pltpu.VMEM((2, w_rows, columns), bf16),
            pltpu.VMEM((2, w_rows, columns), bf16),
            pltpu.VMEM(exponents.shape, jnp.float32),
            pltpu.VMEM((CHUNKS, n_col, piece, depth), bf16),
            pltpu.VMEM((2 * columns // tile_n, depth, tile_n), bf16),
            pltpu.VMEM((CHUNKS, n_row, rows_out, 2 * columns), bf16),
            pltpu.VMEM((CHUNKS, 2, rows_out, 2 * columns), bf16),
            pltpu.VMEM((CHUNKS, 2, rows_out, 2 * columns), bf16),
            pltpu.VMEM((CHUNKS, 2, rows_out, 2 * columns), bf16),
            pltpu.VMEM((CHUNKS, rows_out, 2 * columns), bf16),
            pltpu.SemaphoreType.DMA((2,)),
            pltpu.SemaphoreType.DMA((2, 2)),
            pltpu.SemaphoreType.DMA((CHUNKS, N_AG)),
            pltpu.SemaphoreType.DMA((CHUNKS, N_AG)),
            pltpu.SemaphoreType.DMA((CHUNKS, N_RS)),
            pltpu.SemaphoreType.DMA((CHUNKS, N_RS)),
        ],
        compiler_params=pltpu.CompilerParams(
            collective_id=0, has_side_effects=True, vmem_limit_bytes=60 * 1024 * 1024
        ),
        cost_estimate=pl.CostEstimate(
            flops=2 * n_col * tokens * depth * 2 * columns,
            bytes_accessed=4 * depth * columns,
            transcendentals=tokens * depth,
        ),
    )(gate_pre, up_pre, residual, base_weight, perturb, exponents)


def solution(mesh):
    spec = P("row", "col")
    turned = P("col", "row")
    return jax.shard_map(
        on_device,
        mesh=mesh,
        in_specs=(turned, turned, spec, spec, spec, spec),
        out_specs=(spec, spec),
        check_vma=False,
    )
```

time: 361 us -> 140 us (0.39)
  waiting for transfers between devices: 292 us -> 0 us
  Pallas kernels: 0 us -> 136 us
  matrix products: 37.3 us -> 0 us
  other arithmetic: 17.5 us -> 0 us
  between operations: 13.7 us -> 0.64 us
  local copies, waits for them, and re-layouts: 0.01 us -> 3.74 us
    reduce_scatter x2 -> x0, waiting for transfers between devices: 204 us -> none  [own_rows(): so_far = lax.psum_scatter(so_far, axis, scatter_dimension=0, tiled=True)]
    pallas_call x0 -> x1, Pallas kernels: none -> 136 us  [on_device(): pl.pallas_call(kernel, out_shape=(out, out), in_specs=[any_spec, any_spec...]
    all_gather x1 -> x0, waiting for transfers between devices: 87.9 us -> none  [on_device(): hidden = lax.all_gather(swiglu(gate_pre, up_pre), 'col', axis=0, tiled=True)]
    dot_general x1 -> x0, matrix products: 37.3 us -> none  [on_device(): jnp.dot(hidden, stacked, preferred_element_type=jnp.float32)]
    convert_element_type x3 -> x0, other arithmetic: 16.6 us -> none  [the longest x1 10.9 us: on_device(): plus_weight = (weight_full + shift).astype(jnp.bfloat16)]
    unnamed x2, local copies, waits for them, and re-layouts: 0.01 us -> 3.74 us
  transfers between devices with their start and end apart: 3 -> 0, of which waited for: 3 -> 0; matrix products, arithmetic and copies ran while one was open for 3% -> 0% of each run, Pallas kernels for 0% -> 0%
where the time goes in v1:
time: 140 us
  Pallas kernels  136 us (97%)
  local copies, waits for them, and re-layouts  3.74 us (3%)
    pallas_call x1, Pallas kernels, on_device(): pl.pallas_call(kernel, out_shape=(out, out), in_specs=[any_spec, any_spec...  136 us
    unnamed x2, local copies, waits for them, and re-layouts  3.74 us

profile of v1, /device:TPU:1, one launch (start us, length us, event | category | flops | bytes accessed | tf_op | source)
XLA Modules:
  0.0 140.1 jit_solution(5240934469961089313)
XLA Ops:
  0.6 135.7 %shard_map.77 = (bf16[256,1024]{1,0:T(8,128)(2,1)}, bf16[256,1024]{1,0:T(8,128)(2,1)}) custom-call(bf16[128,3328]{1,0:T(8,128)(2,1)} %gate_hbm.1, bf16[128,3328]{1,0:T(8,128)(2,1)} %up_hbm.1, bf16[256,1024]{1,0:T(8,128)(2,1)} %res_ref.1, bf16[3328,1024]{1,0:T(8,128)(2,1)} %base_hbm.1, bf16[3328,1024]{1,0:T(8,128)(2,1)} %pert_hbm.1, s32[26,1024]{1,0:T(8,128)} %expo_ref.1), custom_call_target="tpu_custom_call" | custom-call | flops 27917287424 | bytes 13631488 | tf_op jit(solution)/shard_map/pallas_call | solution.py:308
  136.3 1.9 %copy.10 = bf16[256,1024]{1,0:T(8,128)(2,1)} copy(bf16[256,1024]{1,0:T(8,128)(2,1)} %get-tuple-element.4) | data formatting | bytes 1048576
  138.2 1.9 %copy.11 = bf16[256,1024]{1,0:T(8,128)(2,1)} copy(bf16[256,1024]{1,0:T(8,128)(2,1)} %get-tuple-element.5) | data formatting | bytes 1048576

commit v2 on v1

v2 whole, which is shorter than its diff:
```python
import functools

import jax
import jax.numpy as jnp
from jax import lax
from jax.experimental import pallas as pl
from jax.experimental.pallas import tpu as pltpu
from jax.sharding import PartitionSpec as P

MESH = pl.DeviceIdType.MESH
STEP_SIZE = 0.25
CHUNKS = 8
TILE_N = 512
W_ROWS = 256
FIRST_AT = 2
NEXT_AT = 1
W_AT = (6, 10)
ZP, Y_AHEAD, Y_BEHIND, OZ_AHEAD, OZ_BEHIND, Y_FAR, OZ_FAR, SIB = range(8)
N_AG = SIB + 8
FAR, MID, NEAR, ZSUM, Z_FIRST, Z_FAR, Z_MID, Z_NEAR = 0, 2, 4, 6, 7, 8, 9, 10
N_RS = 11


def kernel(
    gate_hbm, up_hbm, res_ref, base_hbm, pert_hbm, expo_ref,
    plus_ref, minus_ref,
    gate_buf, up_buf, factor_ref, hid, weight, part,
    far_in, mid_in, near_in, z_in,
    part_z, first_in, z_far_in, z_mid_in, z_near_in,
    in_sem, w_sem, ag_send, ag_recv, rs_send, rs_recv,
):
    tokens, depth = gate_buf.shape
    piece = tokens // CHUNKS
    n_tiles, _, tile_n = weight.shape
    halves = n_tiles // 2
    columns = halves * tile_n
    w_tiles = depth // W_ROWS
    group = depth // expo_ref.shape[0]

    row, col = lax.axis_index("row"), lax.axis_index("col")
    x, zl = row // 2, row % 2
    y, zh, core = col // 4, (col // 2) % 2, col % 2
    step = 2 * core + 3
    back = 5 - 2 * core
    x_ahead, x_behind = (x + step) % 4, (x + back) % 4
    y_ahead, y_behind, y_far = (y + step) % 4, (y + back) % 4, (y + 2) % 4

    def col_of(y_, zh_, core_=core):
        return y_ * 4 + zh_ * 2 + core_

    oz, oc, ozl = 1 - zh, 1 - core, 1 - zl
    zp_dev = (row, col_of(y, oz))
    ya_dev, yb_dev = (row, col_of(y_ahead, zh)), (row, col_of(y_behind, zh))
    sib_dev = (row, col_of(y, zh, oc))
    xa_dev, xb_dev = (x_ahead * 2 + zl, col), (x_behind * 2 + zl, col)
    zl_dev = (x * 2 + ozl, col)

    origins = [
        (y, zh), (y, oz), (y_behind, zh), (y_ahead, zh),
        (y_behind, oz), (y_ahead, oz), (y_far, zh), (y_far, oz),
    ]

    in_copies = [
        pltpu.make_async_copy(gate_hbm, gate_buf, in_sem.at[0]),
        pltpu.make_async_copy(up_hbm, up_buf, in_sem.at[1]),
    ]
    for copy in in_copies:
        copy.start()

    places = ((1, 2), (3, 0))

    def w_copies(i):
        rows = pl.ds(pl.multiple_of(i * W_ROWS, W_ROWS), W_ROWS)
        copies = []
        for half in range(halves):
            cols = pl.ds(half * tile_n, tile_n)
            for j, source in enumerate((base_hbm, pert_hbm)):
                place = places[j][half]
                copies.append(pltpu.make_async_copy(
                    source.at[rows, cols], weight.at[place, rows], w_sem.at[i, place]
                ))
        return copies

    barrier = pltpu.get_barrier_semaphore()
    for dev in (zp_dev, ya_dev, yb_dev, sib_dev, xa_dev, xb_dev, zl_dev):
        pl.semaphore_signal(barrier, inc=1, device_id=dev, device_id_type=MESH)

    @pl.loop(0, w_tiles)
    def _(i):
        for copy in w_copies(i):
            copy.start()

    def ag(k, kind, origin, dev):
        src = hid.at[k, origin]
        return pltpu.make_async_remote_copy(
            src_ref=src, dst_ref=src, send_sem=ag_send.at[k, kind], recv_sem=ag_recv.at[k, kind],
            device_id=dev, device_id_type=MESH,
        )

    def ag_send_piece(k, kind, place, dev):
        ag(k, kind, col_of(*origins[place]), dev).start()

    def ag_wait(k, kind):
        ag(k, kind, 0, sib_dev).wait_recv()

    def to_sibling(k, place):
        ag_send_piece(k, SIB + place, place, sib_dev)

    def across_z(k):
        ag_send_piece(k, ZP, 0, zp_dev)

    def own_along_y(k):
        ag_send_piece(k, Y_AHEAD, 0, ya_dev)
        ag_send_piece(k, Y_BEHIND, 0, yb_dev)

    def other_along_y(k):
        ag_wait(k, ZP)
        ag_send_piece(k, OZ_AHEAD, 1, ya_dev)
        ag_send_piece(k, OZ_BEHIND, 1, yb_dev)
        to_sibling(k, 1)

    def own_onward(k):
        ag_wait(k, Y_AHEAD)
        ag_send_piece(k, Y_FAR, 2, ya_dev)
        to_sibling(k, 2)
        ag_wait(k, Y_BEHIND)
        to_sibling(k, 3)

    def other_onward(k):
        ag_wait(k, OZ_AHEAD)
        ag_send_piece(k, OZ_FAR, 4, ya_dev)
        to_sibling(k, 4)
        ag_wait(k, OZ_BEHIND)
        to_sibling(k, 5)

    def last_to_sibling(k):
        ag_wait(k, Y_FAR)
        to_sibling(k, 6)
        ag_wait(k, OZ_FAR)
        to_sibling(k, 7)

    def all_here(k):
        for place in range(8):
            ag_wait(k, SIB + place)

    def rs(k, kind, src, dst, dev):
        return pltpu.make_async_remote_copy(
            src_ref=src, dst_ref=dst, send_sem=rs_send.at[k, kind], recv_sem=rs_recv.at[k, kind],
            device_id=dev, device_id_type=MESH,
        )

    def rs_copy(k, kind):
        if kind == ZSUM:
            return rs(k, kind, part.at[k, x * 2 + ozl], z_in.at[k], zl_dev)
        if kind == Z_FIRST:
            return rs(k, kind, part_z.at[k, ozl], first_in.at[k], zl_dev)
        if kind > Z_FIRST:
            dest, dst, dev = {
                Z_FAR: ((x + 2) % 4, z_far_in, xa_dev),
                Z_MID: (x_ahead, z_mid_in, xa_dev),
                Z_NEAR: (x_behind, z_near_in, xb_dev),
            }[kind]
            return rs(k, kind, part_z.at[k, zl, dest], dst.at[k], dev)
        lo = kind % 2
        dest, dst, dev = {
            FAR: ((x + 2) % 4, far_in, xa_dev),
            MID: (x_ahead, mid_in, xa_dev),
            NEAR: (x_behind, near_in, xb_dev),
        }[kind - lo]
        return rs(k, kind, part.at[k, dest * 2 + lo], dst.at[k, lo], dev)

    def f32(value):
        return value.astype(jnp.float32)

    def send_raw(k):
        for kind in (FAR, FAR + 1, NEAR, NEAR + 1):
            rs_copy(k, kind).start()

    def pair_sum(k, dest):
        return f32(part_z[k, zl, dest]) + f32(first_in[k, dest])

    def reduce_first(k):
        rs_copy(k, Z_FIRST).wait_recv()
        for kind, dest in ((Z_FAR, (x + 2) % 4), (Z_NEAR, x_behind)):
            part_z[k, zl, dest] = pair_sum(k, dest).astype(jnp.bfloat16)
            rs_copy(k, kind).start()

    def reduce_mid(k):
        for lo in range(2):
            rs_copy(k, FAR + lo).wait_recv()
            dest = x_ahead * 2 + lo
            part[k, dest] = (f32(part[k, dest]) + f32(far_in[k, lo])).astype(jnp.bfloat16)
            rs_copy(k, MID + lo).start()
        rs_copy(k, Z_FAR).wait_recv()
        total = pair_sum(k, x_ahead) + f32(z_far_in[k])
        part_z[k, zl, x_ahead] = total.astype(jnp.bfloat16)
        rs_copy(k, Z_MID).start()

    def reduce_z(k):
        for lo in range(2):
            rs_copy(k, NEAR + lo).wait_recv()
            rs_copy(k, MID + lo).wait_recv()
        dest = x * 2 + ozl
        total = f32(part[k, dest]) + f32(mid_in[k, ozl]) + f32(near_in[k, ozl])
        part[k, dest] = total.astype(jnp.bfloat16)
        rs_copy(k, ZSUM).start()

    def finish(k):
        for kind in (ZSUM, Z_MID, Z_NEAR):
            rs_copy(k, kind).wait_recv()
        last = columns - tile_n
        for half in range(2):
            rows = pl.ds(half * piece, piece)
            out_rows = pl.ds(pl.multiple_of(half * tokens + k * piece, piece), piece)
            total = f32(part[k, x * 2 + zl, rows]) + f32(mid_in[k, zl, rows])
            total = total + f32(near_in[k, zl, rows]) + f32(z_in[k, rows])
            stream = f32(res_ref[out_rows])
            plus_ref[out_rows] = (stream + total[:, :columns]).astype(jnp.bfloat16)
            minus_ref[out_rows, :last] = (stream[:, :last] + total[:, columns:]).astype(jnp.bfloat16)
            total = f32(part_z[k, zl, x, rows]) + f32(first_in[k, x, rows])
            total = total + f32(z_mid_in[k, rows]) + f32(z_near_in[k, rows])
            minus_ref[out_rows, last:] = (stream[:, last:] + total).astype(jnp.bfloat16)

    for copy in in_copies:
        copy.wait()

    def make_hidden(k):
        rows = pl.ds(pl.multiple_of(k * piece, piece), piece)
        gate, up = f32(gate_buf[rows]), f32(up_buf[rows])
        hid[k, col] = (gate / (1.0 + jnp.exp(-gate)) * up).astype(jnp.bfloat16)

    make_hidden(0)
    pl.semaphore_wait(barrier, 7)
    across_z(0)
    own_along_y(0)
    to_sibling(0, 0)

    @pl.loop(1, CHUNKS)
    def _(k):
        make_hidden(k)
        across_z(k)
        to_sibling(k, 0)

    other_along_y(0)
    factor_ref[...] = STEP_SIZE * jnp.exp2(expo_ref[...].astype(jnp.float32))

    @pl.loop(0, w_tiles)
    def _(i):
        for copy in w_copies(i):
            copy.wait()
        for g in range(W_ROWS // group):
            rows = pl.ds(pl.multiple_of(i * W_ROWS + g * group, group), group)
            factor = factor_ref[pl.ds(i * (W_ROWS // group) + g, 1)]
            for half in range(halves):
                plus_at, minus_at = places[0][half], places[1][half]
                scale = factor[:, half * tile_n:(half + 1) * tile_n]
                base = f32(weight[plus_at, rows])
                shift = scale * f32(weight[minus_at, rows])
                weight[plus_at, rows] = (base + shift).astype(jnp.bfloat16)
                weight[minus_at, rows] = (base - shift).astype(jnp.bfloat16)

        @pl.when(i == W_AT[0])
        def _():
            own_onward(0)

        @pl.when(i == W_AT[1])
        def _():
            other_onward(0)
            own_along_y(1)
            other_along_y(1)
            own_along_y(2)

    last_to_sibling(0)

    @pl.loop(0, CHUNKS)
    def _(k):
        all_here(k)
        more = k + 1 < CHUNKS

        def product(n):
            lhs = hid[k].reshape(hid.shape[1] * piece, depth)
            out = jnp.dot(lhs, weight[n], preferred_element_type=jnp.float32)
            return out.astype(jnp.bfloat16).reshape(part.shape[1], part.shape[2], tile_n)

        out = product(0)
        for dest in range(part.shape[1]):
            part_z[k, dest % 2, dest // 2] = out[dest]
        rs_copy(k, Z_FIRST).start()

        @pl.loop(1, n_tiles)
        def _(n):
            cols = pl.ds(pl.multiple_of((n - 1) * tile_n, tile_n), tile_n)
            part[k, :, :, cols] = product(n)

            @pl.when((n == FIRST_AT) & (k == 0))
            def _():
                own_onward(1)

            @pl.when((n == jnp.where(k == 0, n_tiles - 1, NEXT_AT)) & more)
            def _():
                other_onward(k + 1)

            @pl.when((n == jnp.where(k == 0, n_tiles - 1, NEXT_AT)) & (k + 2 < CHUNKS))
            def _():
                other_along_y(k + 2)

            @pl.when((n == jnp.where(k == 0, n_tiles - 1, NEXT_AT)) & (k + 3 < CHUNKS))
            def _():
                own_along_y(k + 3)

        send_raw(k)

        @pl.when(k + 2 < CHUNKS)
        def _():
            own_onward(k + 2)

        reduce_first(k)

        @pl.when(k >= 1)
        def _():
            reduce_mid(k - 1)

        @pl.when(more)
        def _():
            last_to_sibling(k + 1)

        @pl.when(k >= 2)
        def _():
            reduce_z(k - 2)

        @pl.when(k >= 3)
        def _():
            finish(k - 3)

    reduce_mid(CHUNKS - 1)
    reduce_z(CHUNKS - 2)
    finish(CHUNKS - 3)
    reduce_z(CHUNKS - 1)
    finish(CHUNKS - 2)
    finish(CHUNKS - 1)

    @pl.loop(0, CHUNKS)
    def _(k):
        for kind in range(N_AG):
            ag(k, kind, 0, sib_dev).wait_send()
        for kind in range(N_RS):
            rs_copy(k, kind).wait_send()


def on_device(gate_pre, up_pre, residual, base_weight, perturb, exponents):
    tokens, depth = gate_pre.shape
    columns = base_weight.shape[1]
    n_col, n_row = 16, 8
    piece = tokens // CHUNKS
    bf16 = jnp.bfloat16
    out = jax.ShapeDtypeStruct(residual.shape, bf16)
    any_spec = pl.BlockSpec(memory_space=pl.ANY)
    vmem_spec = pl.BlockSpec(memory_space=pltpu.VMEM)
    wide = 2 * columns - TILE_N
    rows_out = n_col // n_row * piece
    return pl.pallas_call(
        kernel,
        out_shape=(out, out),
        in_specs=[any_spec, any_spec, vmem_spec, any_spec, any_spec, vmem_spec],
        out_specs=(vmem_spec, vmem_spec),
        scratch_shapes=[
            pltpu.VMEM((tokens, depth), bf16),
            pltpu.VMEM((tokens, depth), bf16),
            pltpu.VMEM(exponents.shape, jnp.float32),
            pltpu.VMEM((CHUNKS, n_col, piece, depth), bf16),
            pltpu.VMEM((2 * columns // TILE_N, depth, TILE_N), bf16),
            pltpu.VMEM((CHUNKS, n_row, rows_out, wide), bf16),
            pltpu.VMEM((CHUNKS, 2, rows_out, wide), bf16),
            pltpu.VMEM((CHUNKS, 2, rows_out, wide), bf16),
            pltpu.VMEM((CHUNKS, 2, rows_out, wide), bf16),
            pltpu.VMEM((CHUNKS, rows_out, wide), bf16),
            pltpu.VMEM((CHUNKS, 2, n_row // 2, rows_out, TILE_N), bf16),
            pltpu.VMEM((CHUNKS, n_row // 2, rows_out, TILE_N), bf16),
            pltpu.VMEM((CHUNKS, rows_out, TILE_N), bf16),
            pltpu.VMEM((CHUNKS, rows_out, TILE_N), bf16),
            pltpu.VMEM((CHUNKS, rows_out, TILE_N), bf16),
            pltpu.SemaphoreType.DMA((2,)),
            pltpu.SemaphoreType.DMA((depth // W_ROWS, 2 * columns // TILE_N)),
            pltpu.SemaphoreType.DMA((CHUNKS, N_AG)),
            pltpu.SemaphoreType.DMA((CHUNKS, N_AG)),
            pltpu.SemaphoreType.DMA((CHUNKS, N_RS)),
            pltpu.SemaphoreType.DMA((CHUNKS, N_RS)),
        ],
        compiler_params=pltpu.CompilerParams(
            collective_id=0, has_side_effects=True, vmem_limit_bytes=60 * 1024 * 1024
        ),
        cost_estimate=pl.CostEstimate(
            flops=2 * n_col * tokens * depth * 2 * columns,
            bytes_accessed=4 * depth * columns,
            transcendentals=tokens * depth,
        ),
    )(gate_pre, up_pre, residual, base_weight, perturb, exponents)


def solution(mesh):
    spec = P("row", "col")
    turned = P("col", "row")
    return jax.shard_map(
        on_device,
        mesh=mesh,
        in_specs=(turned, turned, spec, spec, spec, spec),
        out_specs=(spec, spec),
        check_vma=False,
    )
```

time: 140 us -> 113 us (0.81)
  Pallas kernels: 136 us -> 108 us
    pallas_call x1, Pallas kernels: 136 us -> 108 us  [on_device(): pl.pallas_call(kernel, out_shape=(out, out), in_specs=[any_spec, any_spec...]
where the time goes in v2:
time: 113 us; the launch traced here: 112 us
  Pallas kernels  108 us (96%)
  local copies, waits for them, and re-layouts  3.74 us (3%)
    pallas_call x1, Pallas kernels, on_device(): pl.pallas_call(kernel, out_shape=(out, out), in_specs=[any_spec, any_spec...  108 us
    unnamed x2, local copies, waits for them, and re-layouts  3.74 us

profile of v2, /device:TPU:1, one launch (start us, length us, event | category | flops | bytes accessed | tf_op | source)
XLA Modules:
  0.0 112.4 jit_solution(4362927596928265520)
XLA Ops:
  0.6 108.1 %shard_map.77 = (bf16[256,1024]{1,0:T(8,128)(2,1)}, bf16[256,1024]{1,0:T(8,128)(2,1)}) custom-call(bf16[128,3328]{1,0:T(8,128)(2,1)} %gate_hbm.1, bf16[128,3328]{1,0:T(8,128)(2,1)} %up_hbm.1, bf16[256,1024]{1,0:T(8,128)(2,1)} %res_ref.1, bf16[3328,1024]{1,0:T(8,128)(2,1)} %base_hbm.1, bf16[3328,1024]{1,0:T(8,128)(2,1)} %pert_hbm.1, s32[26,1024]{1,0:T(8,128)} %expo_ref.1), custom_call_target="tpu_custom_call" | custom-call | flops 27917287424 | bytes 13631488 | tf_op jit(solution)/shard_map/pallas_call | solution.py:361
  108.7 1.9 %copy.10 = bf16[256,1024]{1,0:T(8,128)(2,1)} copy(bf16[256,1024]{1,0:T(8,128)(2,1)} %get-tuple-element.4) | data formatting | bytes 1048576
  110.6 1.9 %copy.11 = bf16[256,1024]{1,0:T(8,128)(2,1)} copy(bf16[256,1024]{1,0:T(8,128)(2,1)} %get-tuple-element.5) | data formatting | bytes 1048576

commit v3 on v0

v3 whole, which is shorter than its diff:
```python
import jax
import jax.numpy as jnp
from jax import lax
from jax.experimental import pallas as pl
from jax.experimental.pallas import tpu as pltpu
from jax.sharding import PartitionSpec as P

MESH = pl.DeviceIdType.MESH
STEP_SIZE = 0.25
CHUNKS = 8
X_TILES = ((0, 512), (512, 1280))
Z_TILE = (1280, 2048)
W_ROWS = 256
FIRST_AT = 1
LEAD_EARLY = True
W_AT = (8, 11)
ZP, Y_AHEAD, Y_BEHIND, Y_FAR, SIB = range(5)
FAR, MID, NEAR, ZSUM, Z_FIRST, Z_FAR, Z_MID, Z_NEAR = range(8)


def kernel(
    gate_hbm, up_hbm, res_hbm, base_hbm, pert_hbm, expo_hbm,
    plus_hbm, minus_hbm,
    gate_buf, up_buf, res_ref, expo_ref, plus_ref, minus_ref, factor_ref, hid, weight, part, part_z,
    far_in, mid_in, near_in, z_in, first_in, z_far_in, z_mid_in, z_near_in,
    in_sem, out_sem, w_sem, ag_send, ag_recv, rs_send, rs_recv,
):
    tokens, depth = gate_buf.shape
    piece = tokens // CHUNKS
    columns = weight.shape[1] // 2
    wide, wide_z = part.shape[-1], part_z.shape[-1]
    w_tiles = depth // W_ROWS
    group = depth // expo_ref.shape[0]

    row, col = lax.axis_index("row"), lax.axis_index("col")
    x, zl = row // 2, row % 2
    y, zh, core = col // 4, (col // 2) % 2, col % 2
    step = 2 * core + 3
    back = 5 - 2 * core
    x_ahead, x_behind, x_far = (x + step) % 4, (x + back) % 4, (x + 2) % 4
    y_ahead, y_behind, y_far = (y + step) % 4, (y + back) % 4, (y + 2) % 4
    oz, oc, ozl = 1 - zh, 1 - core, 1 - zl

    def col_of(y_, zh_, core_):
        return y_ * 4 + zh_ * 2 + core_

    zp_dev = (row, col_of(y, oz, core))
    ya_dev, yb_dev = (row, col_of(y_ahead, zh, core)), (row, col_of(y_behind, zh, core))
    sib_dev = (row, col_of(y, zh, oc))
    xa_dev, xb_dev = (x_ahead * 2 + zl, col), (x_behind * 2 + zl, col)
    zl_dev = (x * 2 + ozl, col)

    head, rest = pl.ds(0, piece), pl.ds(piece, tokens - piece)
    in_copies = [
        pltpu.make_async_copy(gate_hbm.at[head], gate_buf.at[head], in_sem.at[0]),
        pltpu.make_async_copy(up_hbm.at[head], up_buf.at[head], in_sem.at[1]),
        pltpu.make_async_copy(gate_hbm.at[rest], gate_buf.at[rest], in_sem.at[2]),
        pltpu.make_async_copy(up_hbm.at[rest], up_buf.at[rest], in_sem.at[3]),
        pltpu.make_async_copy(expo_hbm, expo_ref, in_sem.at[4]),
        pltpu.make_async_copy(res_hbm, res_ref, in_sem.at[5]),
    ]

    def w_copies(i):
        rows = pl.ds(pl.multiple_of(i * W_ROWS, W_ROWS), W_ROWS)
        return [
            pltpu.make_async_copy(
                source.at[rows], weight.at[rows, pl.ds(j * columns, columns)], w_sem.at[i, j]
            )
            for j, source in enumerate((base_hbm, pert_hbm))
        ]

    barrier = pltpu.get_barrier_semaphore()
    for dev in (zp_dev, ya_dev, yb_dev, sib_dev, xa_dev, xb_dev, zl_dev):
        pl.semaphore_signal(barrier, inc=1, device_id=dev, device_id_type=MESH)
    for copy in in_copies:
        copy.start()

    @pl.loop(0, w_tiles)
    def _(i):
        for copy in w_copies(i):
            copy.start()

    def ag(src, k, kind, dev):
        return pltpu.make_async_remote_copy(
            src_ref=src, dst_ref=src, send_sem=ag_send.at[kind // SIB], recv_sem=ag_recv.at[k, kind],
            device_id=dev, device_id_type=MESH,
        )

    def single(k, y_, zh_):
        return hid.at[k, core, y_ * 2 + zh_]

    def pair(k, y_):
        return hid.at[k, core, pl.ds(y_ * 2, 2)]

    def to_sibling(k, y_):
        ag(pair(k, y_), k, SIB, sib_dev).start()

    def across_z(k):
        ag(single(k, y, zh), k, ZP, zp_dev).start()

    def along_y(k):
        ag(single(k, y, oz), k, ZP, zp_dev).wait_recv()
        ag(pair(k, y), k, Y_AHEAD, ya_dev).start()
        ag(pair(k, y), k, Y_BEHIND, yb_dev).start()
        to_sibling(k, y)

    def onward(k):
        ag(pair(k, y_behind), k, Y_AHEAD, ya_dev).wait_recv()
        ag(pair(k, y_behind), k, Y_FAR, ya_dev).start()
        to_sibling(k, y_behind)
        ag(pair(k, y_ahead), k, Y_BEHIND, yb_dev).wait_recv()
        to_sibling(k, y_ahead)

    def last_to_sibling(k):
        ag(pair(k, y_far), k, Y_FAR, ya_dev).wait_recv()
        to_sibling(k, y_far)

    def all_here(k):
        ag(hid.at[k, oc], k, SIB, sib_dev).wait_recv()

    def rs_copy(k, kind):
        if kind == ZSUM:
            src, dst, dev = part.at[k, x * 2 + ozl], z_in, zl_dev
        elif kind == Z_FIRST:
            src, dst, dev = part_z.at[k, ozl], first_in, zl_dev
        elif kind > Z_FIRST:
            dest, dst, dev = {
                Z_FAR: (x_far, z_far_in, xa_dev),
                Z_MID: (x_ahead, z_mid_in, xa_dev),
                Z_NEAR: (x_behind, z_near_in, xb_dev),
            }[kind]
            src = part_z.at[k, zl, dest]
        else:
            dest, dst, dev = {
                FAR: (x_far, far_in, xa_dev),
                MID: (x_ahead, mid_in, xa_dev),
                NEAR: (x_behind, near_in, xb_dev),
            }[kind]
            src = part.at[k, pl.ds(dest * 2, 2)]
        return pltpu.make_async_remote_copy(
            src_ref=src, dst_ref=dst.at[k], send_sem=rs_send.at[kind], recv_sem=rs_recv.at[k, kind],
            device_id=dev, device_id_type=MESH,
        )

    def f32(value):
        return value.astype(jnp.float32)

    def pair_sum(k, dest):
        return f32(part_z[k, zl, dest]) + f32(first_in[k, dest])

    def reduce_first(k):
        rs_copy(k, Z_FIRST).wait_recv()
        for kind, dest in ((Z_FAR, x_far), (Z_NEAR, x_behind)):
            part_z[k, zl, dest] = pair_sum(k, dest).astype(jnp.bfloat16)
            rs_copy(k, kind).start()

    def reduce_mid(k):
        rs_copy(k, FAR).wait_recv()
        for lo in range(2):
            dest = x_ahead * 2 + lo
            part[k, dest] = (f32(part[k, dest]) + f32(far_in[k, lo])).astype(jnp.bfloat16)
        rs_copy(k, MID).start()

    def reduce_z_mid(k):
        rs_copy(k, Z_FAR).wait_recv()
        total = pair_sum(k, x_ahead) + f32(z_far_in[k])
        part_z[k, zl, x_ahead] = total.astype(jnp.bfloat16)
        rs_copy(k, Z_MID).start()

    def reduce_z(k):
        rs_copy(k, NEAR).wait_recv()
        rs_copy(k, MID).wait_recv()
        dest = x * 2 + ozl
        total = f32(part[k, dest]) + f32(mid_in[k, ozl]) + f32(near_in[k, ozl])
        part[k, dest] = total.astype(jnp.bfloat16)
        rs_copy(k, ZSUM).start()

    def finish(k):
        for kind in (Z_MID, Z_NEAR, ZSUM):
            rs_copy(k, kind).wait_recv()
        last = wide - columns
        for half in range(2):
            out_rows = pl.ds(pl.multiple_of(half * tokens + k * piece, piece), piece)
            total = f32(part[k, x * 2 + zl, half]) + f32(mid_in[k, zl, half])
            total = total + f32(near_in[k, zl, half]) + f32(z_in[k, half])
            stream = f32(res_ref[out_rows])
            plus_ref[out_rows] = (stream + total[:, :columns]).astype(jnp.bfloat16)
            minus_ref[out_rows, :last] = (stream[:, :last] + total[:, columns:]).astype(jnp.bfloat16)
            total = f32(part_z[k, zl, x, half]) + f32(first_in[k, x, half])
            total = total + f32(z_mid_in[k, half]) + f32(z_near_in[k, half])
            minus_ref[out_rows, last:] = (stream[:, last:] + total).astype(jnp.bfloat16)
        for copy in out_copies(k):
            copy.start()

    def out_copies(k):
        copies = []
        for half in range(2):
            rows = pl.ds(pl.multiple_of(half * tokens + k * piece, piece), piece)
            for j, (src, dst) in enumerate(((plus_ref, plus_hbm), (minus_ref, minus_hbm))):
                copies.append(pltpu.make_async_copy(src.at[rows], dst.at[rows], out_sem.at[k, half * 2 + j]))
        return copies

    def make_hidden(k):
        rows = pl.ds(pl.multiple_of(k * piece, piece), piece)
        gate, up = f32(gate_buf[rows]), f32(up_buf[rows])
        hid[k, core, y * 2 + zh] = (gate / (1.0 + jnp.exp(-gate)) * up).astype(jnp.bfloat16)

    for copy in in_copies[:2]:
        copy.wait()
    make_hidden(0)
    pl.semaphore_wait(barrier, 7)
    across_z(0)
    ag(single(0, y, zh), 0, Y_AHEAD, ya_dev).start()
    ag(single(0, y, zh), 0, Y_BEHIND, yb_dev).start()

    for copy in in_copies[2:4]:
        copy.wait()

    @pl.loop(1, CHUNKS)
    def _(k):
        make_hidden(k)
        across_z(k)

    ag(single(0, y, oz), 0, ZP, zp_dev).wait_recv()
    ag(single(0, y, oz), 0, Y_AHEAD, ya_dev).start()
    ag(single(0, y, oz), 0, Y_BEHIND, yb_dev).start()
    to_sibling(0, y)
    for copy in in_copies[4:]:
        copy.wait()
    factor_ref[...] = STEP_SIZE * jnp.exp2(expo_ref[...].astype(jnp.float32))

    @pl.loop(0, w_tiles)
    def _(i):
        for copy in w_copies(i):
            copy.wait()
        for g in range(W_ROWS // group):
            rows = pl.ds(pl.multiple_of(i * W_ROWS + g * group, group), group)
            factor = factor_ref[pl.ds(i * (W_ROWS // group) + g, 1)]
            left, right = slice(0, columns), slice(columns, 2 * columns)
            base = f32(weight[rows, left])
            shift = factor * f32(weight[rows, right])
            weight[rows, left] = (base + shift).astype(jnp.bfloat16)
            weight[rows, right] = (base - shift).astype(jnp.bfloat16)

        @pl.when(i == W_AT[0])
        def _():
            onward(0)
            along_y(1)

        @pl.when(i == W_AT[1])
        def _():
            if LEAD_EARLY:
                along_y(2)

    last_to_sibling(0)

    @pl.loop(0, CHUNKS)
    def _(k):
        all_here(k)
        more = k + 1 < CHUNKS

        def product(span):
            lhs = hid[k].reshape(2 * part.shape[1] * piece, depth)
            out = jnp.dot(lhs, weight[:, slice(*span)], preferred_element_type=jnp.float32)
            return out.astype(jnp.bfloat16).reshape(2, part.shape[1], piece, span[1] - span[0])

        for n, span in enumerate(X_TILES):
            out = product(span)
            for half in range(2):
                part[k, :, half, :, slice(*span)] = out[half]

            if n == FIRST_AT:
                @pl.when(k == 0)
                def _():
                    onward(1)
                    along_y(3)

        rs_copy(k, FAR).start()
        rs_copy(k, NEAR).start()
        out = product(Z_TILE)
        for half in range(2):
            for dest in range(part.shape[1]):
                part_z[k, dest % 2, dest // 2, half] = out[half, dest]
        rs_copy(k, Z_FIRST).start()

        @pl.when(k >= 1)
        def _():
            reduce_first(k - 1)

        @pl.when(k + 2 < CHUNKS)
        def _():
            onward(k + 2)

        @pl.when(k + 4 < CHUNKS)
        def _():
            along_y(k + 4)

        @pl.when(more)
        def _():
            last_to_sibling(k + 1)

        @pl.when(k >= 1)
        def _():
            reduce_mid(k - 1)

        @pl.when(k >= 2)
        def _():
            reduce_z_mid(k - 2)
            reduce_z(k - 2)

        @pl.when(k >= 3)
        def _():
            finish(k - 3)

    reduce_z_mid(CHUNKS - 2)
    reduce_mid(CHUNKS - 1)
    reduce_first(CHUNKS - 1)
    reduce_z(CHUNKS - 2)
    finish(CHUNKS - 3)
    reduce_z_mid(CHUNKS - 1)
    reduce_z(CHUNKS - 1)
    finish(CHUNKS - 2)
    finish(CHUNKS - 1)

    @pl.loop(0, CHUNKS)
    def _(k):
        for copy in out_copies(k):
            copy.wait()

    def sent(src, sem):
        pltpu.make_async_remote_copy(
            src_ref=src, dst_ref=src, send_sem=sem, recv_sem=ag_recv.at[0, 0],
            device_id=sib_dev, device_id_type=MESH,
        ).wait_send()

    sent(hid.at[:, 0, pl.ds(0, 7)], ag_send.at[0])
    sent(hid.at[:, 0], ag_send.at[1])
    for kind in (FAR, MID, NEAR):
        sent(part.at[:, pl.ds(0, 2)], rs_send.at[kind])
    sent(part.at[:, 0], rs_send.at[ZSUM])
    sent(part_z.at[:, 0], rs_send.at[Z_FIRST])
    for kind in (Z_FAR, Z_MID, Z_NEAR):
        sent(part_z.at[:, 0, 0], rs_send.at[kind])


def on_device(gate_pre, up_pre, residual, base_weight, perturb, exponents):
    tokens, depth = gate_pre.shape
    columns = base_weight.shape[1]
    n_col, n_row = 16, 8
    piece = tokens // CHUNKS
    wide, wide_z = Z_TILE[0], Z_TILE[1] - Z_TILE[0]
    bf16 = jnp.bfloat16
    out = jax.ShapeDtypeStruct(residual.shape, bf16)
    any_spec = pl.BlockSpec(memory_space=pl.ANY)
    block, block_z = (2, piece, wide), (2, piece, wide_z)
    return pl.pallas_call(
        kernel,
        out_shape=(out, out),
        in_specs=[any_spec] * 6,
        out_specs=(any_spec, any_spec),
        scratch_shapes=[
            pltpu.VMEM((tokens, depth), bf16),
            pltpu.VMEM((tokens, depth), bf16),
            pltpu.VMEM(residual.shape, bf16),
            pltpu.VMEM(exponents.shape, jnp.int32),
            pltpu.VMEM(residual.shape, bf16),
            pltpu.VMEM(residual.shape, bf16),
            pltpu.VMEM(exponents.shape, jnp.float32),
            pltpu.VMEM((CHUNKS, 2, n_col // 2, piece, depth), bf16),
            pltpu.VMEM((depth, 2 * columns), bf16),
            pltpu.VMEM((CHUNKS, n_row, *block), bf16),
            pltpu.VMEM((CHUNKS, 2, n_row // 2, *block_z), bf16),
            pltpu.VMEM((CHUNKS, 2, *block), bf16),
            pltpu.VMEM((CHUNKS, 2, *block), bf16),
            pltpu.VMEM((CHUNKS, 2, *block), bf16),
            pltpu.VMEM((CHUNKS, *block), bf16),
            pltpu.VMEM((CHUNKS, n_row // 2, *block_z), bf16),
            pltpu.VMEM((CHUNKS, *block_z), bf16),
            pltpu.VMEM((CHUNKS, *block_z), bf16),
            pltpu.VMEM((CHUNKS, *block_z), bf16),
            pltpu.SemaphoreType.DMA((6,)),
            pltpu.SemaphoreType.DMA((CHUNKS, 4)),
            pltpu.SemaphoreType.DMA((depth // W_ROWS, 2)),
            pltpu.SemaphoreType.DMA((2,)),
            pltpu.SemaphoreType.DMA((CHUNKS, 5)),
            pltpu.SemaphoreType.DMA((8,)),
            pltpu.SemaphoreType.DMA((CHUNKS, 8)),
        ],
        compiler_params=pltpu.CompilerParams(
            collective_id=0, has_side_effects=True, vmem_limit_bytes=60 * 1024 * 1024
        ),
        cost_estimate=pl.CostEstimate(
            flops=2 * n_col * tokens * depth * 2 * columns,
            bytes_accessed=4 * depth * columns,
            transcendentals=tokens * depth,
        ),
    )(gate_pre, up_pre, residual, base_weight, perturb, exponents)


def solution(mesh):
    spec = P("row", "col")
    turned = P("col", "row")
    return jax.shard_map(
        on_device,
        mesh=mesh,
        in_specs=(turned, turned, spec, spec, spec, spec),
        out_specs=(spec, spec),
        check_vma=False,
    )
```

time: 361 us -> 103 us (0.29)
  waiting for transfers between devices: 292 us -> 0 us
  Pallas kernels: 0 us -> 98.9 us
  matrix products: 37.3 us -> 0 us
  other arithmetic: 17.5 us -> 0 us
  between operations: 13.7 us -> 0.64 us
  local copies, waits for them, and re-layouts: 0.01 us -> 3.74 us
    reduce_scatter x2 -> x0, waiting for transfers between devices: 204 us -> none  [own_rows(): so_far = lax.psum_scatter(so_far, axis, scatter_dimension=0, tiled=True)]
    pallas_call x0 -> x1, Pallas kernels: none -> 98.9 us  [on_device(): pl.pallas_call(kernel, out_shape=(out, out), in_specs=[any_spec] * 6, out...]
    all_gather x1 -> x0, waiting for transfers between devices: 87.9 us -> none  [on_device(): hidden = lax.all_gather(swiglu(gate_pre, up_pre), 'col', axis=0, tiled=True)]
    dot_general x1 -> x0, matrix products: 37.3 us -> none  [on_device(): jnp.dot(hidden, stacked, preferred_element_type=jnp.float32)]
    convert_element_type x3 -> x0, other arithmetic: 16.6 us -> none  [the longest x1 10.9 us: on_device(): plus_weight = (weight_full + shift).astype(jnp.bfloat16)]
    unnamed x2, local copies, waits for them, and re-layouts: 0.01 us -> 3.74 us
  transfers between devices with their start and end apart: 3 -> 0, of which waited for: 3 -> 0; matrix products, arithmetic and copies ran while one was open for 3% -> 0% of each run, Pallas kernels for 0% -> 0%
where the time goes in v3:
time: 103 us
  Pallas kernels  98.9 us (96%)
  local copies, waits for them, and re-layouts  3.74 us (4%)
    pallas_call x1, Pallas kernels, on_device(): pl.pallas_call(kernel, out_shape=(out, out), in_specs=[any_spec] * 6, out...  98.9 us
    unnamed x2, local copies, waits for them, and re-layouts  3.74 us

profile of v3, /device:TPU:1, one launch (start us, length us, event | category | flops | bytes accessed | tf_op | source)
XLA Modules:
  0.0 103.2 jit_solution(4833437396166765840)
XLA Ops:
  0.6 98.9 %shard_map.77 = (bf16[256,1024]{1,0:T(8,128)(2,1)}, bf16[256,1024]{1,0:T(8,128)(2,1)}) custom-call(bf16[128,3328]{1,0:T(8,128)(2,1)} %gate_hbm.1, bf16[128,3328]{1,0:T(8,128)(2,1)} %up_hbm.1, bf16[256,1024]{1,0:T(8,128)(2,1)} %res_hbm.1, bf16[3328,1024]{1,0:T(8,128)(2,1)} %base_hbm.1, bf16[3328,1024]{1,0:T(8,128)(2,1)} %pert_hbm.1, s32[26,1024]{1,0:T(8,128)} %expo_hbm.1), custom_call_target="tpu_custom_call" | custom-call | flops 27917287424 | bytes 13631488 | tf_op jit(solution)/shard_map/pallas_call | solution.py:356
  99.5 1.9 %copy.10 = bf16[256,1024]{1,0:T(8,128)(2,1)} copy(bf16[256,1024]{1,0:T(8,128)(2,1)} %get-tuple-element.4) | data formatting | bytes 1048576
  101.4 1.9 %copy.11 = bf16[256,1024]{1,0:T(8,128)(2,1)} copy(bf16[256,1024]{1,0:T(8,128)(2,1)} %get-tuple-element.5) | data formatting | bytes 1048576

commit v4 on v3

--- a/solution.py
+++ b/solution.py
@@ -8,8 +8,8 @@
 MESH = pl.DeviceIdType.MESH
 STEP_SIZE = 0.25
 CHUNKS = 8
-X_TILES = ((0, 512), (512, 1280))
-Z_TILE = (1280, 2048)
+X_TILES = ((0, 512), (512, 1152))
+Z_TILE = (1152, 2048)
 W_ROWS = 256
 FIRST_AT = 1
 LEAD_EARLY = True
@@ -20,8 +20,8 @@
 
 def kernel(
     gate_hbm, up_hbm, res_hbm, base_hbm, pert_hbm, expo_hbm,
-    plus_hbm, minus_hbm,
-    gate_buf, up_buf, res_ref, expo_ref, plus_ref, minus_ref, factor_ref, hid, weight, part, part_z,
+    out_hbm,
+    gate_buf, up_buf, res_ref, expo_ref, out_ref, factor_ref, hid, weight, part, part_z,
     far_in, mid_in, near_in, z_in, first_in, z_far_in, z_mid_in, z_near_in,
     in_sem, out_sem, w_sem, ag_send, ag_recv, rs_send, rs_recv,
 ):
@@ -184,11 +184,11 @@
             total = f32(part[k, x * 2 + zl, half]) + f32(mid_in[k, zl, half])
             total = total + f32(near_in[k, zl, half]) + f32(z_in[k, half])
             stream = f32(res_ref[out_rows])
-            plus_ref[out_rows] = (stream + total[:, :columns]).astype(jnp.bfloat16)
-            minus_ref[out_rows, :last] = (stream[:, :last] + total[:, columns:]).astype(jnp.bfloat16)
+            out_ref[out_rows, :columns] = (stream + total[:, :columns]).astype(jnp.bfloat16)
+            out_ref[out_rows, columns:wide] = (stream[:, :last] + total[:, columns:]).astype(jnp.bfloat16)
             total = f32(part_z[k, zl, x, half]) + f32(first_in[k, x, half])
             total = total + f32(z_mid_in[k, half]) + f32(z_near_in[k, half])
-            minus_ref[out_rows, last:] = (stream[:, last:] + total).astype(jnp.bfloat16)
+            out_ref[out_rows, wide:] = (stream[:, last:] + total).astype(jnp.bfloat16)
         for copy in out_copies(k):
             copy.start()
 
@@ -196,8 +196,7 @@
         copies = []
         for half in range(2):
             rows = pl.ds(pl.multiple_of(half * tokens + k * piece, piece), piece)
-            for j, (src, dst) in enumerate(((plus_ref, plus_hbm), (minus_ref, minus_hbm))):
-                copies.append(pltpu.make_async_copy(src.at[rows], dst.at[rows], out_sem.at[k, half * 2 + j]))
+            copies.append(pltpu.make_async_copy(out_ref.at[rows], out_hbm.at[rows], out_sem.at[k, half]))
         return copies
 
     def make_hidden(k):
@@ -277,6 +276,14 @@
 
         rs_copy(k, FAR).start()
         rs_copy(k, NEAR).start()
+        @pl.when(k + 2 < CHUNKS)
+        def _():
+            onward(k + 2)
+
+        @pl.when(k + 4 < CHUNKS)
+        def _():
+            along_y(k + 4)
+
         out = product(Z_TILE)
         for half in range(2):
             for dest in range(part.shape[1]):
@@ -287,14 +294,6 @@
         def _():
             reduce_first(k - 1)
 
-        @pl.when(k + 2 < CHUNKS)
-        def _():
-            onward(k + 2)
-
-        @pl.when(k + 4 < CHUNKS)
-        def _():
-            along_y(k + 4)
-
         @pl.when(more)
         def _():
             last_to_sibling(k + 1)
@@ -312,13 +311,13 @@
         def _():
             finish(k - 3)
 
+    reduce_mid(CHUNKS - 1)
     reduce_z_mid(CHUNKS - 2)
-    reduce_mid(CHUNKS - 1)
+    reduce_z(CHUNKS - 2)
     reduce_first(CHUNKS - 1)
-    reduce_z(CHUNKS - 2)
     finish(CHUNKS - 3)
+    reduce_z(CHUNKS - 1)
     reduce_z_mid(CHUNKS - 1)
-    reduce_z(CHUNKS - 1)
     finish(CHUNKS - 2)
     finish(CHUNKS - 1)
 
@@ -350,21 +349,20 @@
     piece = tokens // CHUNKS
     wide, wide_z = Z_TILE[0], Z_TILE[1] - Z_TILE[0]
     bf16 = jnp.bfloat16
-    out = jax.ShapeDtypeStruct(residual.shape, bf16)
+    out = jax.ShapeDtypeStruct((residual.shape[0], 2 * columns), bf16)
     any_spec = pl.BlockSpec(memory_space=pl.ANY)
     block, block_z = (2, piece, wide), (2, piece, wide_z)
-    return pl.pallas_call(
+    both = pl.pallas_call(
         kernel,
-        out_shape=(out, out),
+        out_shape=out,
         in_specs=[any_spec] * 6,
-        out_specs=(any_spec, any_spec),
+        out_specs=any_spec,
         scratch_shapes=[
             pltpu.VMEM((tokens, depth), bf16),
             pltpu.VMEM((tokens, depth), bf16),
             pltpu.VMEM(residual.shape, bf16),
             pltpu.VMEM(exponents.shape, jnp.int32),
-            pltpu.VMEM(residual.shape, bf16),
-            pltpu.VMEM(residual.shape, bf16),
+            pltpu.VMEM(out.shape, bf16),
             pltpu.VMEM(exponents.shape, jnp.float32),
             pltpu.VMEM((CHUNKS, 2, n_col // 2, piece, depth), bf16),
             pltpu.VMEM((depth, 2 * columns), bf16),
@@ -379,7 +377,7 @@
             pltpu.VMEM((CHUNKS, *block_z), bf16),
             pltpu.VMEM((CHUNKS, *block_z), bf16),
             pltpu.SemaphoreType.DMA((6,)),
-            pltpu.SemaphoreType.DMA((CHUNKS, 4)),
+            pltpu.SemaphoreType.DMA((CHUNKS, 2)),
             pltpu.SemaphoreType.DMA((depth // W_ROWS, 2)),
             pltpu.SemaphoreType.DMA((2,)),
             pltpu.SemaphoreType.DMA((CHUNKS, 5)),
@@ -395,6 +393,7 @@
             transcendentals=tokens * depth,
         ),
     )(gate_pre, up_pre, residual, base_weight, perturb, exponents)
+    return both[:, :columns], both[:, columns:]
 
 
 def solution(mesh):

time: 103 us -> 98.9 us (0.960)
  Pallas kernels: 98.9 us -> 95.8 us
  local copies, waits for them, and re-layouts: 3.74 us -> 2.24 us
    unnamed x2 -> x0, local copies, waits for them, and re-layouts: 3.74 us -> none
    pallas_call x1, Pallas kernels: 98.9 us -> 95.8 us  [on_device(): pl.pallas_call(kernel, out_shape=out, in_specs=[any_spec] * 6, out_specs=...]
    slice x0 -> x1, local copies, waits for them, and re-layouts: none -> 2.24 us  [on_device(): return (both[:, :columns], both[:, columns:])]
where the time goes in v4:
time: 98.9 us; the launch traced here: 98.6 us
  Pallas kernels  95.8 us (97%)
  local copies, waits for them, and re-layouts  2.24 us (2%)
    pallas_call x1, Pallas kernels, on_device(): pl.pallas_call(kernel, out_shape=out, in_specs=[any_spec] * 6, out_specs=...  95.8 us
    slice x1, local copies, waits for them, and re-layouts, on_device(): return (both[:, :columns], both[:, columns:])  2.24 us

profile of v4, /device:TPU:1, one launch (start us, length us, event | category | flops | bytes accessed | tf_op | source)
XLA Modules:
  0.0 98.6 jit_solution(16977224484596760946)
XLA Ops:
  0.6 95.8 %shard_map.77 = bf16[256,2048]{1,0:T(8,128)(2,1)} custom-call(bf16[128,3328]{1,0:T(8,128)(2,1)} %gate_hbm.1, bf16[128,3328]{1,0:T(8,128)(2,1)} %up_hbm.1, bf16[256,1024]{1,0:T(8,128)(2,1)} %res_hbm.1, bf16[3328,1024]{1,0:T(8,128)(2,1)} %base_hbm.1, bf16[3328,1024]{1,0:T(8,128)(2,1)} %pert_hbm.1, s32[26,1024]{1,0:T(8,128)} %expo_hbm.1), custom_call_target="tpu_custom_call" | custom-call | flops 27917287424 | bytes 13631488 | tf_op jit(solution)/shard_map/pallas_call | solution.py:355
  96.4 2.2 %fusion = (bf16[256,1024]{1,0:T(8,128)(2,1)}, bf16[256,1024]{1,0:T(8,128)(2,1)}) fusion(bf16[256,2048]{1,0:T(8,128)(2,1)} %shard_map.77), kind=kLoop, calls=%fused_computation | loop fusion | bytes 2097152 | tf_op jit(solution)/shard_map/slice | solution.py:396

commit v5 on v4

--- a/solution.py
+++ b/solution.py
@@ -11,10 +11,9 @@
 X_TILES = ((0, 512), (512, 1152))
 Z_TILE = (1152, 2048)
 W_ROWS = 256
-FIRST_AT = 1
-LEAD_EARLY = True
-W_AT = (8, 11)
-ZP, Y_AHEAD, Y_BEHIND, Y_FAR, SIB = range(5)
+FIRST_AT = 0
+W_AT = (5, 9)
+ZP, Y_AHEAD, Y_BEHIND, Y_FAR, SIB, FIRST_OTHER = range(6)
 FAR, MID, NEAR, ZSUM, Z_FIRST, Z_FAR, Z_MID, Z_NEAR = range(8)
 
 
@@ -82,7 +81,7 @@
 
     def ag(src, k, kind, dev):
         return pltpu.make_async_remote_copy(
-            src_ref=src, dst_ref=src, send_sem=ag_send.at[kind // SIB], recv_sem=ag_recv.at[k, kind],
+            src_ref=src, dst_ref=src, send_sem=ag_send.at[kind == SIB and 1 or 0], recv_sem=ag_recv.at[k, kind],
             device_id=dev, device_id_type=MESH,
         )
 
@@ -185,7 +184,8 @@
             total = total + f32(near_in[k, zl, half]) + f32(z_in[k, half])
             stream = f32(res_ref[out_rows])
             out_ref[out_rows, :columns] = (stream + total[:, :columns]).astype(jnp.bfloat16)
-            out_ref[out_rows, columns:wide] = (stream[:, :last] + total[:, columns:]).astype(jnp.bfloat16)
+            if last:
+                out_ref[out_rows, columns:wide] = (stream[:, :last] + total[:, columns:]).astype(jnp.bfloat16)
             total = f32(part_z[k, zl, x, half]) + f32(first_in[k, x, half])
             total = total + f32(z_mid_in[k, half]) + f32(z_near_in[k, half])
             out_ref[out_rows, wide:] = (stream[:, last:] + total).astype(jnp.bfloat16)
@@ -221,7 +221,7 @@
         across_z(k)
 
     ag(single(0, y, oz), 0, ZP, zp_dev).wait_recv()
-    ag(single(0, y, oz), 0, Y_AHEAD, ya_dev).start()
+    ag(single(0, y, oz), 0, FIRST_OTHER, ya_dev).start()
     ag(single(0, y, oz), 0, Y_BEHIND, yb_dev).start()
     to_sibling(0, y)
     for copy in in_copies[4:]:
@@ -243,13 +243,18 @@
 
         @pl.when(i == W_AT[0])
         def _():
-            onward(0)
+            ag(single(0, y_behind, zh), 0, Y_AHEAD, ya_dev).wait_recv()
+            ag(single(0, y_behind, zh), 0, Y_FAR, ya_dev).start()
+
+        @pl.when(i == W_AT[1])
+        def _():
+            ag(single(0, y_behind, oz), 0, FIRST_OTHER, ya_dev).wait_recv()
+            ag(single(0, y_behind, oz), 0, Y_FAR, ya_dev).start()
             along_y(1)
-
-        @pl.when(i == W_AT[1])
-        def _():
-            if LEAD_EARLY:
-                along_y(2)
+            to_sibling(0, y_behind)
+            ag(pair(0, y_ahead), 0, Y_BEHIND, yb_dev).wait_recv()
+            to_sibling(0, y_ahead)
+            along_y(2)
 
     last_to_sibling(0)
 
@@ -290,13 +295,13 @@
                 part_z[k, dest % 2, dest // 2, half] = out[half, dest]
         rs_copy(k, Z_FIRST).start()
 
+        @pl.when(more)
+        def _():
+            last_to_sibling(k + 1)
+
         @pl.when(k >= 1)
         def _():
             reduce_first(k - 1)
-
-        @pl.when(more)
-        def _():
-            last_to_sibling(k + 1)
 
         @pl.when(k >= 1)
         def _():
@@ -380,7 +385,7 @@
             pltpu.SemaphoreType.DMA((CHUNKS, 2)),
             pltpu.SemaphoreType.DMA((depth // W_ROWS, 2)),
             pltpu.SemaphoreType.DMA((2,)),
-            pltpu.SemaphoreType.DMA((CHUNKS, 5)),
+            pltpu.SemaphoreType.DMA((CHUNKS, 6)),
             pltpu.SemaphoreType.DMA((8,)),
             pltpu.SemaphoreType.DMA((CHUNKS, 8)),
         ],

time: 98.9 us -> 97.1 us (0.982); the launches traced: 98.6 us -> 95.8 us
  Pallas kernels: 95.8 us -> 93 us
    pallas_call x1, Pallas kernels: 95.8 us -> 93 us  [on_device(): pl.pallas_call(kernel, out_shape=out, in_specs=[any_spec] * 6, out_specs=...]
where the time goes in v5:
time: 97.1 us; the launch traced here: 95.8 us
  Pallas kernels  93 us (96%)
  local copies, waits for them, and re-layouts  2.24 us (2%)
    pallas_call x1, Pallas kernels, on_device(): pl.pallas_call(kernel, out_shape=out, in_specs=[any_spec] * 6, out_specs=...  93 us
    slice x1, local copies, waits for them, and re-layouts, on_device(): return (both[:, :columns], both[:, columns:])  2.24 us

profile of v5, /device:TPU:1, one launch (start us, length us, event | category | flops | bytes accessed | tf_op | source)
XLA Modules:
  0.0 95.8 jit_solution(6854191757342364597)
XLA Ops:
  0.6 93.0 %shard_map.77 = bf16[256,2048]{1,0:T(8,128)(2,1)} custom-call(bf16[128,3328]{1,0:T(8,128)(2,1)} %gate_hbm.1, bf16[128,3328]{1,0:T(8,128)(2,1)} %up_hbm.1, bf16[256,1024]{1,0:T(8,128)(2,1)} %res_hbm.1, bf16[3328,1024]{1,0:T(8,128)(2,1)} %base_hbm.1, bf16[3328,1024]{1,0:T(8,128)(2,1)} %pert_hbm.1, s32[26,1024]{1,0:T(8,128)} %expo_hbm.1), custom_call_target="tpu_custom_call" | custom-call | flops 27917287424 | bytes 13631488 | tf_op jit(solution)/shard_map/pallas_call | solution.py:360
  93.6 2.2 %fusion = (bf16[256,1024]{1,0:T(8,128)(2,1)}, bf16[256,1024]{1,0:T(8,128)(2,1)}) fusion(bf16[256,2048]{1,0:T(8,128)(2,1)} %shard_map.77), kind=kLoop, calls=%fused_computation | loop fusion | bytes 2097152 | tf_op jit(solution)/shard_map/slice | solution.py:401

commit v6 on v5

--- a/solution.py
+++ b/solution.py
@@ -8,7 +8,7 @@
 MESH = pl.DeviceIdType.MESH
 STEP_SIZE = 0.25
 CHUNKS = 8
-X_TILES = ((0, 512), (512, 1152))
+X_TILES = ((0, 640), (640, 1152))
 Z_TILE = (1152, 2048)
 W_ROWS = 256
 FIRST_AT = 0
@@ -295,6 +295,10 @@
                 part_z[k, dest % 2, dest // 2, half] = out[half, dest]
         rs_copy(k, Z_FIRST).start()
 
+        @pl.when(k >= 1)
+        def _():
+            reduce_mid(k - 1)
+
         @pl.when(more)
         def _():
             last_to_sibling(k + 1)
@@ -302,10 +306,6 @@
         @pl.when(k >= 1)
         def _():
             reduce_first(k - 1)
-
-        @pl.when(k >= 1)
-        def _():
-            reduce_mid(k - 1)
 
         @pl.when(k >= 2)
         def _():

time: 97.1 us -> 97.2 us (level)
  no operation moved by 1% of the time
where the time goes in v6:
time: 97.2 us; the launch traced here: 96.2 us
  Pallas kernels  93.3 us (96%)
  local copies, waits for them, and re-layouts  2.24 us (2%)
    pallas_call x1, Pallas kernels, on_device(): pl.pallas_call(kernel, out_shape=out, in_specs=[any_spec] * 6, out_specs=...  93.3 us
    slice x1, local copies, waits for them, and re-layouts, on_device(): return (both[:, :columns], both[:, columns:])  2.24 us

profile of v6, /device:TPU:1, one launch (start us, length us, event | category | flops | bytes accessed | tf_op | source)
XLA Modules:
  0.0 96.2 jit_solution(12998907600238742231)
XLA Ops:
  0.6 93.3 %shard_map.77 = bf16[256,2048]{1,0:T(8,128)(2,1)} custom-call(bf16[128,3328]{1,0:T(8,128)(2,1)} %gate_hbm.1, bf16[128,3328]{1,0:T(8,128)(2,1)} %up_hbm.1, bf16[256,1024]{1,0:T(8,128)(2,1)} %res_hbm.1, bf16[3328,1024]{1,0:T(8,128)(2,1)} %base_hbm.1, bf16[3328,1024]{1,0:T(8,128)(2,1)} %pert_hbm.1, s32[26,1024]{1,0:T(8,128)} %expo_hbm.1), custom_call_target="tpu_custom_call" | custom-call | flops 27917287424 | bytes 13631488 | tf_op jit(solution)/shard_map/pallas_call | solution.py:360
  93.9 2.2 %fusion = (bf16[256,1024]{1,0:T(8,128)(2,1)}, bf16[256,1024]{1,0:T(8,128)(2,1)}) fusion(bf16[256,2048]{1,0:T(8,128)(2,1)} %shard_map.77), kind=kLoop, calls=%fused_computation | loop fusion | bytes 2097152 | tf_op jit(solution)/shard_map/slice | solution.py:401
